TPU v7x, 32 devices: a whole 2x2x4 slice. The times are simulated.
32 devices in a mesh: seq: 4 (over x, core), fsdp: 8 (over z, y).
Axes of the slice: x: 2, y: 2, z: 4, core: 2. Of those that a mesh axis runs over, the one named last changes fastest.
Arguments:
- image_tokens: bfloat16 [8, 1024, 1536], P('fsdp', 'seq'), may hold values from -6 to 6
- text_tokens: bfloat16 [8, 160, 1536], P('fsdp', 'seq'), may hold values from -6 to 6
- condition: bfloat16 [8, 1536], P('fsdp'), may hold values from -6 to 6
- occupied: int32 [8], P('fsdp'), may hold values 0 or 1
- image_cotangent: bfloat16 [8, 1024, 1536], P('fsdp', 'seq'), may hold values from -6 to 6
- text_cotangent: bfloat16 [8, 160, 1536], P('fsdp', 'seq'), may hold values from -6 to 6
- image_modulator: bfloat16 [1, 1536, 9216], P(None, 'fsdp'), may hold values from -0.15625 to 0.15625
- image_heads: bfloat16 [1, 1536, 4608], P(None, 'fsdp'), may hold values from -0.21875 to 0.21875
- image_merge: bfloat16 [1, 1536, 1536], P(None, 'fsdp'), may hold values from -0.3125 to 0.3125
- image_expand: bfloat16 [1, 1536, 6144], P(None, 'fsdp'), may hold values from -0.15625 to 0.15625
- image_reduce: bfloat16 [1, 6144, 1536], P(None, 'fsdp'), may hold values from -0.078125 to 0.078125
- text_modulator: bfloat16 [1, 1536, 9216], P(None, 'fsdp'), may hold values from -0.15625 to 0.15625
- text_heads: bfloat16 [1, 1536, 4608], P(None, 'fsdp'), may hold values from -0.21875 to 0.21875
- text_merge: bfloat16 [1, 1536, 1536], P(None, 'fsdp'), may hold values from -0.3125 to 0.3125
- text_expand: bfloat16 [1, 1536, 6144], P(None, 'fsdp'), may hold values from -0.15625 to 0.15625
- text_reduce: bfloat16 [1, 6144, 1536], P(None, 'fsdp'), may hold values from -0.078125 to 0.078125
Outputs:
- image_output: bfloat16 [8, 1024, 1536], P('fsdp', 'seq')
- text_output: bfloat16 [8, 160, 1536], P('fsdp', 'seq')
- image_input_grad: bfloat16 [8, 1024, 1536], P('fsdp', 'seq')
- text_input_grad: bfloat16 [8, 160, 1536], P('fsdp', 'seq')
- condition_grad: float32 [8, 1536], P('fsdp')
- image_modulator_grad: float32 [1, 1536, 9216], P(None, 'fsdp')
- image_heads_grad: float32 [1, 1536, 4608], P(None, 'fsdp')
- image_merge_grad: float32 [1, 1536, 1536], P(None, 'fsdp')
- image_expand_grad: float32 [1, 1536, 6144], P(None, 'fsdp')
- image_reduce_grad: float32 [1, 6144, 1536], P(None, 'fsdp')
- text_modulator_grad: float32 [1, 1536, 9216], P(None, 'fsdp')
- text_heads_grad: float32 [1, 1536, 4608], P(None, 'fsdp')
- text_merge_grad: float32 [1, 1536, 1536], P(None, 'fsdp')
- text_expand_grad: float32 [1, 1536, 6144], P(None, 'fsdp')
- text_reduce_grad: float32 [1, 6144, 1536], P(None, 'fsdp')
All inputs are finite; a program needn't handle non-finite values. No bound on the sum of `occupied` on one device may be relied on, other than what follows from the above.
Results may differ from a plain program's by a relative error of at most 0.02.
The roundings to bfloat16 on the way count: a program that leaves them out, or rounds other values in their place, can miss the bound.
Values may be sent and summed in bfloat16 or wider, within the bound.
No kernel may reach another device: no remote copies, remote signals or barrier semaphores. Data moves between devices by JAX's collectives and lax.ppermute only.
A program may use at most 448 MiB of HBM per device.

v0:
```python
import jax
import jax.numpy as jnp
from jax import lax
from jax.sharding import PartitionSpec as P

HEAD_DIM = 64
EPSILON = 1e-06


def layer_norm(values):
    centered = values - jnp.mean(values, axis=-1, keepdims=True)
    inverse = lax.rsqrt(jnp.mean(centered * centered, axis=-1, keepdims=True) + EPSILON)
    return (centered * inverse, inverse)


def norm_back(incoming, normed, inverse):
    mean_plain = jnp.mean(incoming, axis=-1, keepdims=True)
    mean_mixed = jnp.mean(incoming * normed, axis=-1, keepdims=True)
    return inverse * (incoming - mean_plain - normed * mean_mixed)


def product(former, latter):
    return jnp.dot(former, latter, preferred_element_type=jnp.float32)


def product_nt(former, latter):
    return lax.dot_general(
        former, latter, (((1,), (1,)), ((), ())), preferred_element_type=jnp.float32
    )


def product_tn(former, latter):
    return lax.dot_general(
        former, latter, (((0,), (0,)), ((), ())), preferred_element_type=jnp.float32
    )


def gelu_tanh(values):
    return jax.nn.gelu(values, approximate=True)


def reduce_rows(former, latter):
    return lax.psum_scatter(
        product_tn(former, latter).astype(jnp.bfloat16), "fsdp", scatter_dimension=0, tiled=True
    ).astype(jnp.float32)


def collect(weights, layer_index):
    return (
        lax.all_gather(weights[0][layer_index], "fsdp", axis=0, tiled=True),
        lax.all_gather(weights[1][layer_index], "fsdp", axis=0, tiled=True),
        lax.all_gather(weights[2][layer_index], "fsdp", axis=0, tiled=True),
        lax.all_gather(weights[3][layer_index], "fsdp", axis=0, tiled=True),
        lax.all_gather(weights[4][layer_index], "fsdp", axis=0, tiled=True),
        lax.all_gather(weights[5][layer_index], "fsdp", axis=0, tiled=True),
        lax.all_gather(weights[6][layer_index], "fsdp", axis=0, tiled=True),
        lax.all_gather(weights[7][layer_index], "fsdp", axis=0, tiled=True),
    )


def head_forward(items):
    query_head, key_head, value_head = items
    scores = product_nt(query_head, key_head) * HEAD_DIM ** (-0.5)
    highest = jnp.max(scores, axis=-1, keepdims=True)
    exponent = jnp.exp(scores - highest)
    totals = jnp.sum(exponent, axis=-1, keepdims=True)
    logsum = highest + jnp.log(totals)
    output = product((exponent / totals).astype(jnp.bfloat16), value_head).astype(jnp.bfloat16)
    return (output, logsum)


def head_backward(items):
    query_head, key_head, value_head, output_grad, logsum = items
    score_scale = HEAD_DIM ** (-0.5)
    scores = product_nt(query_head, key_head) * score_scale
    probs = jnp.exp(scores - logsum)
    probs_grad = product_nt(output_grad, value_head)
    value_grad = product_tn(probs.astype(jnp.bfloat16), output_grad)
    scores_grad = (
        probs * (probs_grad - jnp.sum(probs * probs_grad, axis=-1, keepdims=True))
    ).astype(jnp.bfloat16)
    query_grad = product(scores_grad, key_head) * score_scale
    key_grad = product_tn(scores_grad, query_head) * score_scale
    return (query_grad, key_grad, value_grad)


def per_device(
    image_tokens,
    text_tokens,
    condition,
    occupied,
    image_cotangent,
    text_cotangent,
    image_modulator,
    image_heads,
    image_merge,
    image_expand,
    image_reduce,
    text_modulator,
    text_heads,
    text_merge,
    text_expand,
    text_reduce,
):
    splits = lax.axis_size("seq")
    layers = image_heads.shape[0]
    model_width = condition.shape[1]
    image_count = image_tokens.shape[1]
    token_count = image_count + text_tokens.shape[1]
    head_slab = model_width // splits
    local_heads = head_slab // HEAD_DIM
    occupancy = occupied.astype(jnp.float32)[0]
    weights = (
        image_heads,
        image_merge,
        image_expand,
        image_reduce,
        text_heads,
        text_merge,
        text_expand,
        text_reduce,
    )
    condition_value = condition.astype(jnp.float32)
    condition_act = jax.nn.silu(condition_value).astype(jnp.bfloat16)
    every_condition = lax.all_gather(condition_act, "fsdp", axis=0, tiled=True)
    own_width = image_modulator.shape[1]
    own_first = lax.axis_index("fsdp") * own_width
    condition_slice = lax.dynamic_slice_in_dim(every_condition, own_first, own_width, 1)
    image_part = jnp.einsum(
        "fr,lrk->flk", condition_slice, image_modulator, preferred_element_type=jnp.float32
    )
    text_part = jnp.einsum(
        "fr,lrk->flk", condition_slice, text_modulator, preferred_element_type=jnp.float32
    )
    image_mod, text_mod = (
        lax.psum_scatter(image_part, "fsdp", scatter_dimension=0, tiled=True),
        lax.psum_scatter(text_part, "fsdp", scatter_dimension=0, tiled=True),
    )
    modulation = (image_mod[0], text_mod[0])
    hidden = [image_tokens[0].astype(jnp.float32), text_tokens[0].astype(jnp.float32)]
    layer_index = 0
    gathered = collect(weights, layer_index)
    portions = [jnp.split(modulation[stream][layer_index], 6) for stream in range(2)]
    first_norm = [layer_norm(hidden[stream]) for stream in range(2)]
    entries = [
        (first_norm[stream][0] * (1.0 + portions[stream][1]) + portions[stream][0]).astype(
            jnp.bfloat16
        )
        for stream in range(2)
    ]
    projected = jnp.concatenate(
        [
            product(entries[stream], gathered[4 * stream]).astype(jnp.bfloat16)
            for stream in range(2)
        ],
        0,
    )
    regrouped = lax.all_to_all(
        projected.reshape(token_count, 3, splits, head_slab),
        "seq",
        split_axis=2,
        concat_axis=0,
        tiled=True,
    )
    regrouped = regrouped.reshape(splits * token_count, 3, local_heads, HEAD_DIM)
    queries = jnp.moveaxis(regrouped[:, 0], 1, 0)
    all_keys = jnp.moveaxis(regrouped[:, 1], 1, 0)
    all_values = jnp.moveaxis(regrouped[:, 2], 1, 0)
    head_outputs, logsum = lax.map(head_forward, (queries, all_keys, all_values))
    attended = jnp.moveaxis(head_outputs, 0, 1)
    returned = lax.all_to_all(
        attended.reshape(splits * token_count, 1, head_slab),
        "seq",
        split_axis=0,
        concat_axis=1,
        tiled=True,
    )
    returned = returned.reshape(token_count, model_width)
    pieces = (returned[:image_count], returned[image_count:])
    stream_records = []
    for stream in range(2):
        portion = portions[stream]
        branch = product(pieces[stream], gathered[4 * stream + 1])
        middle = hidden[stream] + portion[2] * branch
        second_norm, second_inverse = layer_norm(middle)
        entry_mlp = (second_norm * (1.0 + portion[4]) + portion[3]).astype(jnp.bfloat16)
        pre_gelu = product(entry_mlp, gathered[4 * stream + 2])
        active = gelu_tanh(pre_gelu).astype(jnp.bfloat16)
        final_out = product(active, gathered[4 * stream + 3])
        hidden[stream] = middle + portion[5] * final_out
        stream_records.append(
            (
                first_norm[stream][0],
                first_norm[stream][1],
                entries[stream],
                pieces[stream],
                branch,
                second_norm,
                second_inverse,
                entry_mlp,
                pre_gelu,
                active,
                final_out,
            )
        )
    records = [(stream_records, queries, all_keys, all_values, logsum)]
    flowing = [
        image_cotangent[0].astype(jnp.float32) * occupancy,
        text_cotangent[0].astype(jnp.float32) * occupancy,
    ]
    mod_grads = [None] * layers
    weight_grads = [None] * layers
    for layer_index in reversed(range(layers)):
        gathered = collect(weights, layer_index)
        stream_records, queries, all_keys, all_values, logsum = records[layer_index]
        portions = [jnp.split(modulation[stream][layer_index], 6) for stream in range(2)]
        terms = [None] * 8
        middle_grads = []
        back_pieces = []
        partial_mods = []
        for stream in range(2):
            (
                normed,
                inverse,
                entry,
                piece,
                branch,
                second_norm,
                second_inverse,
                entry_mlp,
                pre_gelu,
                active,
                final_out,
            ) = stream_records[stream]
            portion = portions[stream]
            outer_grad = flowing[stream]
            gate_two = jnp.sum(outer_grad * final_out, axis=0)
            final_grad = (outer_grad * portion[5]).astype(jnp.bfloat16)
            terms[4 * stream + 3] = reduce_rows(active, final_grad)
            active_grad = product_nt(final_grad, gathered[4 * stream + 3])
            pre_grad = jax.vjp(gelu_tanh, pre_gelu)[1](active_grad)[0].astype(jnp.bfloat16)
            terms[4 * stream + 2] = reduce_rows(entry_mlp, pre_grad)
            entry_grad = product_nt(pre_grad, gathered[4 * stream + 2])
            scale_two = jnp.sum(entry_grad * second_norm, axis=0)
            shift_two = jnp.sum(entry_grad, axis=0)
            middle_grad = outer_grad + norm_back(
                entry_grad * (1.0 + portion[4]), second_norm, second_inverse
            )
            gate_one = jnp.sum(middle_grad * branch, axis=0)
            branch_grad = (middle_grad * portion[2]).astype(jnp.bfloat16)
            terms[4 * stream + 1] = reduce_rows(piece, branch_grad)
            back_pieces.append(
                product_nt(branch_grad, gathered[4 * stream + 1]).astype(jnp.bfloat16)
            )
            middle_grads.append(middle_grad)
            partial_mods.append((gate_one, shift_two, scale_two, gate_two))
        joined_grad = jnp.concatenate(back_pieces, 0).reshape(token_count, splits, head_slab)
        attended_grad = lax.all_to_all(joined_grad, "seq", split_axis=1, concat_axis=0, tiled=True)
        attended_grad = jnp.moveaxis(
            attended_grad.reshape(splits * token_count, local_heads, HEAD_DIM), 1, 0
        )
        queries_grad, keys_grad, values_grad = lax.map(
            head_backward, (queries, all_keys, all_values, attended_grad, logsum)
        )
        stacked = jnp.stack([queries_grad, keys_grad, values_grad], axis=0).astype(jnp.bfloat16)
        stacked = jnp.transpose(stacked, (2, 0, 1, 3)).reshape(
            splits * token_count, 3, 1, head_slab
        )
        projected_grad = lax.all_to_all(
            stacked, "seq", split_axis=0, concat_axis=2, tiled=True
        ).reshape(token_count, 3 * model_width)
        row_parts = (projected_grad[:image_count], projected_grad[image_count:])
        layer_mods = []
        for stream in range(2):
            normed, inverse, entry = (
                stream_records[stream][0],
                stream_records[stream][1],
                stream_records[stream][2],
            )
            portion = portions[stream]
            terms[4 * stream] = reduce_rows(entry, row_parts[stream])
            entry_grad = product_nt(row_parts[stream], gathered[4 * stream])
            scale_one = jnp.sum(entry_grad * normed, axis=0)
            shift_one = jnp.sum(entry_grad, axis=0)
            flowing[stream] = middle_grads[stream] + norm_back(
                entry_grad * (1.0 + portion[1]), normed, inverse
            )
            gate_one, shift_two, scale_two, gate_two = partial_mods[stream]
            layer_mods.append(
                jnp.concatenate([shift_one, scale_one, gate_one, shift_two, scale_two, gate_two])
            )
        mod_grads[layer_index] = layer_mods
        weight_grads[layer_index] = (
            lax.psum(terms[0].astype(jnp.bfloat16), "seq").astype(jnp.float32),
            lax.psum(terms[1].astype(jnp.bfloat16), "seq").astype(jnp.float32),
            lax.psum(terms[2].astype(jnp.bfloat16), "seq").astype(jnp.float32),
            lax.psum(terms[3].astype(jnp.bfloat16), "seq").astype(jnp.float32),
            lax.psum(terms[4].astype(jnp.bfloat16), "seq").astype(jnp.float32),
            lax.psum(terms[5].astype(jnp.bfloat16), "seq").astype(jnp.float32),
            lax.psum(terms[6].astype(jnp.bfloat16), "seq").astype(jnp.float32),
            lax.psum(terms[7].astype(jnp.bfloat16), "seq").astype(jnp.float32),
        )
    image_mod_grad = jnp.stack([mod_grads[0][0]])[None]
    text_mod_grad = jnp.stack([mod_grads[0][1]])[None]
    image_mod_total, text_mod_total = (
        lax.psum(image_mod_grad.astype(jnp.bfloat16), "seq").astype(jnp.float32),
        lax.psum(text_mod_grad.astype(jnp.bfloat16), "seq").astype(jnp.float32),
    )
    image_every, text_every = (
        lax.all_gather(image_mod_total.astype(jnp.bfloat16), "fsdp", axis=0, tiled=True),
        lax.all_gather(text_mod_total.astype(jnp.bfloat16), "fsdp", axis=0, tiled=True),
    )
    image_mod_weight = jnp.einsum(
        "fr,flk->lrk", condition_slice, image_every, preferred_element_type=jnp.float32
    )
    text_mod_weight = jnp.einsum(
        "fr,flk->lrk", condition_slice, text_every, preferred_element_type=jnp.float32
    )
    condition_parts = jnp.einsum(
        "flk,lrk->fr", image_every, image_modulator, preferred_element_type=jnp.float32
    ) + jnp.einsum("flk,lrk->fr", text_every, text_modulator, preferred_element_type=jnp.float32)
    silu_grad = lax.all_to_all(condition_parts, "fsdp", split_axis=0, concat_axis=1, tiled=True)
    sigmoid_value = jax.nn.sigmoid(condition_value)
    condition_grad = silu_grad * sigmoid_value * (1.0 + condition_value * (1.0 - sigmoid_value))

    def stacked_grad(position):
        return jnp.stack([weight_grads[0][position]])

    return (
        (occupancy * hidden[0])[None].astype(jnp.bfloat16),
        (occupancy * hidden[1])[None].astype(jnp.bfloat16),
        flowing[0][None].astype(jnp.bfloat16),
        flowing[1][None].astype(jnp.bfloat16),
        condition_grad,
        image_mod_weight,
        stacked_grad(0),
        stacked_grad(1),
        stacked_grad(2),
        stacked_grad(3),
        text_mod_weight,
        stacked_grad(4),
        stacked_grad(5),
        stacked_grad(6),
        stacked_grad(7),
    )


def solution(mesh):
    placed = (
        P("fsdp", "seq", None),
        P("fsdp", "seq", None),
        P("fsdp", None),
        P("fsdp"),
        P("fsdp", "seq", None),
        P("fsdp", "seq", None),
        P(None, "fsdp", None),
        P(None, "fsdp", None),
        P(None, "fsdp", None),
        P(None, "fsdp", None),
        P(None, "fsdp", None),
        P(None, "fsdp", None),
        P(None, "fsdp", None),
        P(None, "fsdp", None),
        P(None, "fsdp", None),
        P(None, "fsdp", None),
    )
    return jax.shard_map(
        per_device,
        mesh=mesh,
        in_specs=placed,
        out_specs=(
            P("fsdp", "seq", None),
            P("fsdp", "seq", None),
            P("fsdp", "seq", None),
            P("fsdp", "seq", None),
            P("fsdp", None),
            P(None, "fsdp", None),
            P(None, "fsdp", None),
            P(None, "fsdp", None),
            P(None, "fsdp", None),
            P(None, "fsdp", None),
            P(None, "fsdp", None),
            P(None, "fsdp", None),
            P(None, "fsdp", None),
            P(None, "fsdp", None),
            P(None, "fsdp", None),
        ),
        check_vma=False,
    )
```

profile of v0, /device:TPU:0, one launch (start us, length us, event | category | flops | bytes accessed | tf_op | source)
XLA Modules:
  0.0 4345.3 jit_solution(4088864998627911147)
XLA Ops:
  8.7 34.1 all-gather.8
  59.7 61.1 %all-reduce.8.cloned.1.call-done = (f32[8,1,9216]{2,0,1:T(8,128)}, f32[8,1,9216]{2,0,1:T(8,128)}) async-done(((f32[8,1,9216]{2,0,1:T(8,128)}, f32[8,1,9216]{2,0,1:T(8,128)}), (f32[8,1,9216]{2,0,1:T(8,128)}, f32[8,1,9216]{2,0,1:T(8,128)})) %all-reduce.8.cloned.1.call-update) | async-done | bytes 589840
  125.6 191.9 %all-gather.20.cloned.1.call-done = bf16[1,1536,4608]{2,1,0:T(8,128)(2,1)} async-done(((bf16[1,192,4608]{2,1,0:T(8,128)(2,1)}), bf16[1,1536,4608]{2,1,0:T(8,128)(2,1)}) %all-gather.20.cloned.1.call-update) | async-done | bytes 14155792 | tf_op jit(solution)/shard_map/all_gather | solution.py:54
  317.5 8.5 fusion.81
  326.0 187.2 %all-gather.18.cloned.1.call-done = bf16[1,1536,4608]{2,1,0:T(8,128)(2,1)} async-done(((bf16[1,192,4608]{2,1,0:T(8,128)(2,1)}), bf16[1,1536,4608]{2,1,0:T(8,128)(2,1)}) %all-gather.18.cloned.1.call-update) | async-done | bytes 14155792 | tf_op jit(solution)/shard_map/all_gather | solution.py:50
  513.2 9.3 fusion.71
  524.2 5.6 reshape.488
  538.4 32.5 all-to-all-done
  570.8 7.3 copy.63
  578.1 6.4 reshape.489
  595.8 37.9 while.26
  648.4 11.9 all-to-all-done.1
  669.9 5.4 fusion.211
  677.4 277.6 %all-gather.24.cloned.1.call-done = bf16[1,1536,6144]{2,1,0:T(8,128)(2,1)} async-done(((bf16[1,192,6144]{2,1,0:T(8,128)(2,1)}), bf16[1,1536,6144]{2,1,0:T(8,128)(2,1)}) %all-gather.24.cloned.1.call-update) | async-done | bytes 18874384 | tf_op jit(solution)/shard_map/all_gather | solution.py:52
  955.0 11.3 fusion.61
  966.2 352.5 %all-gather.26.cloned.1.call-done = bf16[1,6144,1536]{2,1,0:T(8,128)(2,1)} async-done(((bf16[1,768,1536]{2,1,0:T(8,128)(2,1)}), bf16[1,6144,1536]{2,1,0:T(8,128)(2,1)}) %all-gather.26.cloned.1.call-update) | async-done | bytes 18874384 | tf_op jit(solution)/shard_map/all_gather | solution.py:53
  1318.7 13.7 fusion.80
  1332.5 11.4 multiply_reduce_fusion.1
  1343.9 15.7 fusion.128
  1366.0 34.2 all-gather.28.cloned.1.call-done
  1405.8 356.8 %all-gather.30.cloned.1.call-done = bf16[1,1536,6144]{2,1,0:T(8,128)(2,1)} async-done(((bf16[1,192,6144]{2,1,0:T(8,128)(2,1)}), bf16[1,1536,6144]{2,1,0:T(8,128)(2,1)}) %all-gather.30.cloned.1.call-update) | async-done | bytes 18874384 | tf_op jit(solution)/shard_map/all_gather | solution.py:56
  1762.6 10.9 fusion.53
  1773.5 353.1 %all-gather.32.cloned.1.call-done = bf16[1,6144,1536]{2,1,0:T(8,128)(2,1)} async-done(((bf16[1,768,1536]{2,1,0:T(8,128)(2,1)}), bf16[1,6144,1536]{2,1,0:T(8,128)(2,1)}) %all-gather.32.cloned.1.call-update) | async-done | bytes 18874384 | tf_op jit(solution)/shard_map/all_gather | solution.py:57
  2126.6 13.2 fusion.141
  2139.8 13.7 multiply_reduce_fusion.7
  2154.2 11.8 fusion.181
  2183.9 8.2 all-to-all-done.2
  2198.5 82.7 %while.27 = (s32[]{:T(128)}, bf16[6,1184,64]{1,2,0:T(8,128)(2,1)}, bf16[6,1184,64]{1,2,0:T(8,128)(2,1)}, bf16[6,1184,64]{1,2,0:T(8,128)(2,1)}, bf16[6,1184,64]{2...) while((s32[]{:T(128)}, bf16[6,1184,64]{1,2,0:T(8,128)(2,1)}, ...), condition=%wide.region_20.21_spmd, body=%wide.region_18.20_spmd.sunk | while | flops 908553088 | bytes 44910832 | solution.py:262
  2284.9 7.7 copy.76
  2292.7 45.9 %all_to_all.76 = bf16[1184,3,1,384]{3,1,2,0:T(4,128)(2,1)S(1)} all-to-all(bf16[1184,3,1,384]{3,1,2,0:T(4,128)(2,1)} %copy.76), channel_id=1, replica_groups=mesh['seq'=4,'fsdp'=8] {'seq'}, dimensions={0} | all-to-all | bytes 5455872 | tf_op jit(solution)/shard_map/all_to_all | solution.py:269
  2346.5 11.1 convolution_convert_fusion.5
  2361.6 10.1 convolution_convert_fusion.4
  2371.8 11.3 convolution_convert_fusion.3
  2383.1 12.6 convolution_convert_fusion.2
  2396.0 10.3 convolution_convert_fusion.1
  2407.0 10.8 convolution_convert_fusion
  2418.4 10.9 fusion.174
  2430.0 156.3 %reduce-scatter.11.cloned.1.call-done = bf16[192,4608]{1,0:T(8,128)(2,1)} async-done(((bf16[1536,4608]{1,0:T(8,128)(2,1)}), bf16[192,4608]{1,0:T(8,128)(2,1)}) %reduce-scatter.11.cloned.1.call-update) | async-done | bytes 1769488 | tf_op jit(solution)/shard_map/reduce_scatter | solution.py:43
  2586.3 232.2 %reduce-scatter.19.cloned.1.call-done = bf16[192,4608]{1,0:T(8,128)(2,1)} async-done(((bf16[1536,4608]{1,0:T(8,128)(2,1)}), bf16[192,4608]{1,0:T(8,128)(2,1)}) %reduce-scatter.19.cloned.1.call-update) | async-done | bytes 1769488 | tf_op jit(solution)/shard_map/reduce_scatter | solution.py:43
  2818.5 312.6 %reduce-scatter.15.cloned.1.call-done = bf16[192,6144]{1,0:T(8,128)(2,1)} async-done(((bf16[1536,6144]{1,0:T(8,128)(2,1)}), bf16[192,6144]{1,0:T(8,128)(2,1)}) %reduce-scatter.15.cloned.1.call-update) | async-done | bytes 2359312 | tf_op jit(solution)/shard_map/reduce_scatter | solution.py:43
  3131.1 312.6 %reduce-scatter.17.cloned.1.call-done = bf16[768,1536]{1,0:T(8,128)(2,1)} async-done(((bf16[6144,1536]{1,0:T(8,128)(2,1)}), bf16[768,1536]{1,0:T(8,128)(2,1)}) %reduce-scatter.17.cloned.1.call-update) | async-done | bytes 2359312 | tf_op jit(solution)/shard_map/reduce_scatter | solution.py:43
  3443.7 312.6 %reduce-scatter.23.cloned.1.call-done = bf16[192,6144]{1,0:T(8,128)(2,1)} async-done(((bf16[1536,6144]{1,0:T(8,128)(2,1)}), bf16[192,6144]{1,0:T(8,128)(2,1)}) %reduce-scatter.23.cloned.1.call-update) | async-done | bytes 2359312 | tf_op jit(solution)/shard_map/reduce_scatter | solution.py:43
  3756.3 312.6 %reduce-scatter.25.cloned.1.call-done = bf16[768,1536]{1,0:T(8,128)(2,1)} async-done(((bf16[6144,1536]{1,0:T(8,128)(2,1)}), bf16[768,1536]{1,0:T(8,128)(2,1)}) %reduce-scatter.25.cloned.1.call-update) | async-done | bytes 2359312 | tf_op jit(solution)/shard_map/reduce_scatter | solution.py:43
  4069.6 11.7 fusion.121
  4087.9 16.0 all-reduce.3
  4103.9 31.3 all_gather.51
  4135.2 31.1 all_gather.50
  4187.0 131.6 %all-reduce.10.cloned.1.call-done = (bf16[1,192,4608]{2,1,0:T(8,128)(2,1)}, bf16[1,192,1536]{2,1,0:T(8,128)(2,1)}, bf16[1,192,6144]{2,1,0:T(8,128)(2,1)}, bf16[1...) async-done(((bf16[1,192,4608]{2,1,0:T(8,128)(2,1)}, ...) | async-done | bytes 14155792 | tf_op jit(solution)/shard_map/psum | solution.py:294
  (359 shorter events, 292.4 us)
Async XLA Ops:
  7.2 36.6 copy-start
  7.2 113.7 %all-reduce.8.cloned.1.call-start = ((), (), s32[]{:S(2)}) async-start(), calls=%async_computation.29 | async-start | bytes 1179648
  46.4 271.1 %all-gather.20.cloned.1.call-start = ((), (), s32[]{:S(2)}) async-start(), calls=%async_computation.22 | async-start | bytes 15925248 | tf_op jit(solution)/shard_map/all_gather | solution.py:54
  47.2 466.0 %all-gather.18.cloned.1.call-start = ((), (), s32[]{:S(2)}) async-start(), calls=%async_computation.21 | async-start | bytes 15925248 | tf_op jit(solution)/shard_map/all_gather | solution.py:50
  47.9 622.0 %all-gather.22.cloned.1.call-start = ((), (), s32[]{:S(2)}) async-start(), calls=%async_computation.23 | async-start | bytes 5308416 | tf_op jit(solution)/shard_map/all_gather | solution.py:51
  48.5 906.5 %all-gather.24.cloned.1.call-start = ((), (), s32[]{:S(2)}) async-start(), calls=%async_computation.24 | async-start | bytes 21233664 | tf_op jit(solution)/shard_map/all_gather | solution.py:52
  49.1 1269.7 %all-gather.26.cloned.1.call-start = ((), (), s32[]{:S(2)}) async-start(), calls=%async_computation.25 | async-start | bytes 21233664 | tf_op jit(solution)/shard_map/all_gather | solution.py:53
  49.7 1350.6 %all-gather.28.cloned.1.call-start = ((), (), s32[]{:S(2)}) async-start(), calls=%async_computation.26 | async-start | bytes 5308416 | tf_op jit(solution)/shard_map/all_gather | solution.py:55
  50.4 1712.2 %all-gather.30.cloned.1.call-start = ((), (), s32[]{:S(2)}) async-start(), calls=%async_computation.27 | async-start | bytes 21233664 | tf_op jit(solution)/shard_map/all_gather | solution.py:56
  51.2 2075.4 %all-gather.32.cloned.1.call-start = ((), (), s32[]{:S(2)}) async-start(), calls=%async_computation.28 | async-start | bytes 21233664 | tf_op jit(solution)/shard_map/all_gather | solution.py:57
  123.2 1220.6 %copy-start.35 = (f32[1536]{0:T(1024)}, f32[1536]{0:T(1024)S(1)}, u32[]{:S(2)}) copy-start(f32[1536]{0:T(1024)S(1)} %get-tuple-element.166) | copy-start | bytes 18436
  125.6 200.4 %copy-start.31 = (f32[1536]{0:T(1024)}, f32[1536]{0:T(1024)S(1)}, u32[]{:S(2)}) copy-start(f32[1536]{0:T(1024)S(1)} %get-tuple-element.163) | copy-start | bytes 18436
  533.5 37.3 all-to-all-start
  643.1 17.2 all-to-all-start.1
  647.3 1782.7 %reduce-scatter.13.cloned.1.call-start = ((), (), s32[]{:S(2)}) async-start(), calls=%async_computation.14 | async-start | bytes 5308416 | tf_op jit(solution)/shard_map/reduce_scatter | solution.py:43
  669.9 285.1 %copy-start.36 = (f32[1536]{0:T(1024)S(1)}, f32[1536]{0:T(1024)}, u32[]{:S(2)}) copy-start(f32[1536]{0:T(1024)} %get-tuple-element.170) | copy-start | bytes 18436
  1318.7 13.7 copy-start.5
  1318.7 13.7 copy-start.48
  1318.7 13.7 copy-start.56
  1332.5 11.4 copy-start.25
  1332.5 11.4 copy-start.63
  1343.9 16.8 copy-start.7
  1343.9 16.8 copy-start.44
  1364.3 35.9 copy-start.37
  1365.3 397.2 %copy-start.30 = (f32[1536]{0:T(1024)S(1)}, f32[1536]{0:T(1024)}, u32[]{:S(2)}) copy-start(f32[1536]{0:T(1024)} %get-tuple-element.160) | copy-start | bytes 18436
  1762.6 364.0 %copy-start.33 = (f32[1536]{0:T(1024)S(1)}, f32[1536]{0:T(1024)}, u32[]{:S(2)}) copy-start(f32[1536]{0:T(1024)} %get-tuple-element.159) | copy-start | bytes 18436
  2154.2 11.8 copy-start.38
  2174.9 17.2 all-to-all-start.2
  2179.1 250.9 %reduce-scatter.21.cloned.1.call-start = ((), (), s32[]{:S(2)}) async-start(), calls=%async_computation.18 | async-start | bytes 5308416 | tf_op jit(solution)/shard_map/reduce_scatter | solution.py:43
  2183.8 402.5 %reduce-scatter.11.cloned.1.call-start = ((), (), s32[]{:S(2)}) async-start(), calls=%async_computation.13 | async-start | bytes 15925248 | tf_op jit(solution)/shard_map/reduce_scatter | solution.py:43
  2357.6 460.9 %reduce-scatter.19.cloned.1.call-start = ((), (), s32[]{:S(2)}) async-start(), calls=%async_computation.17 | async-start | bytes 15925248 | tf_op jit(solution)/shard_map/reduce_scatter | solution.py:43
  2371.7 759.4 %reduce-scatter.15.cloned.1.call-start = ((), (), s32[]{:S(2)}) async-start(), calls=%async_computation.15 | async-start | bytes 21233664 | tf_op jit(solution)/shard_map/reduce_scatter | solution.py:43
  2383.1 1060.7 %reduce-scatter.17.cloned.1.call-start = ((), (), s32[]{:S(2)}) async-start(), calls=%async_computation.16 | async-start | bytes 21233664 | tf_op jit(solution)/shard_map/reduce_scatter | solution.py:43
  2395.7 1360.5 %reduce-scatter.23.cloned.1.call-start = ((), (), s32[]{:S(2)}) async-start(), calls=%async_computation.19 | async-start | bytes 21233664 | tf_op jit(solution)/shard_map/reduce_scatter | solution.py:43
  2406.3 1662.6 %reduce-scatter.25.cloned.1.call-start = ((), (), s32[]{:S(2)}) async-start(), calls=%async_computation.20 | async-start | bytes 21233664 | tf_op jit(solution)/shard_map/reduce_scatter | solution.py:43
  2417.8 1900.8 %all-reduce.10.cloned.1.call-start = ((), (), s32[]{:S(2)}) async-start(), calls=%async_computation.30 | async-start | bytes 28311552 | tf_op jit(solution)/shard_map/psum | solution.py:294
  4069.6 12.3 copy-start.61
  4069.6 12.9 copy-start.60
  4069.6 13.5 copy-start.58
  4069.6 14.1 copy-start.57
  4069.6 14.7 copy-start.59
  4069.6 15.9 copy-start.67
  4069.6 16.5 copy-start.65
  4069.6 17.1 copy-start.64
  4069.6 17.7 copy-start.66
  4103.9 63.4 %copy-start.3 = (bf16[1,192,9216]{2,1,0:T(8,128)(2,1)S(1)}, bf16[1,192,9216]{2,1,0:T(8,128)(2,1)}, u32[]{:S(2)}) copy-start(bf16[1,192,9216]{2,1,0:T(8,128)(2,1)} %param.26) | copy-start | bytes 10616836
  4135.2 33.2 copy-start.21
  4169.0 15.9 all-to-all-start.4
  (48 other events, 177.4 us)
Sparse Core Ops, SparseCore 0:
  46.5 74.3 all-reduce.7
  123.1 194.3 all-gather.19
  319.7 193.4 all-gather.17
  515.2 77.4 all-gather.21
  594.2 360.7 all-gather.23
  956.3 362.3 all-gather.25
  1320.9 79.2 all-gather.27
  1401.8 360.7 all-gather.29
  1764.1 362.4 all-gather.31
  2130.6 95.6 reduce-scatter.12
  2230.5 95.2 reduce-scatter.20
  2357.7 228.6 reduce-scatter.10
  2590.0 228.4 reduce-scatter.18
  2822.2 308.8 reduce-scatter.14
  3134.8 308.8 reduce-scatter.16
  3447.4 308.7 reduce-scatter.22
  3760.0 308.8 reduce-scatter.24
  4071.9 246.6 all-reduce.9
where the time goes:
time: 4360 us; the launch traced here: 4350 us
  waiting for transfers between devices  3640 us (83%)
  matrix products  349 us (8%)
  blocking collectives  158 us (4%)
  local copies, waits for them, and re-layouts  102 us (2%)
  other arithmetic  58 us (1%)
    reduce_scatter x8, waiting for transfers between devices, reduce_rows(): lax.psum_scatter(product_tn(former, latter).astype(jnp.bfloat16), 'fsdp',...  1640 us
    all_gather x1, waiting for transfers between devices, collect(): lax.all_gather(weights[6][layer_index], 'fsdp', axis=0, tiled=True)  357 us
    all_gather x1, waiting for transfers between devices, collect(): lax.all_gather(weights[7][layer_index], 'fsdp', axis=0, tiled=True)  353 us
    all_gather x1, waiting for transfers between devices, collect(): lax.all_gather(weights[3][layer_index], 'fsdp', axis=0, tiled=True)  353 us
    all_gather x1, waiting for transfers between devices, collect(): lax.all_gather(weights[2][layer_index], 'fsdp', axis=0, tiled=True)  278 us
    all_gather x1, waiting for transfers between devices, collect(): lax.all_gather(weights[4][layer_index], 'fsdp', axis=0, tiled=True)  192 us
    all_gather x1, waiting for transfers between devices, collect(): lax.all_gather(weights[0][layer_index], 'fsdp', axis=0, tiled=True)  187 us
    psum x1, waiting for transfers between devices, per_device(): lax.psum(terms[0].astype(jnp.bfloat16), 'seq').astype(jnp.float32)  132 us
  transfers between devices with their start and end apart: 22, of which 18 were waited for; matrix products, arithmetic and copies ran while one was open for 11% of the time, Pallas kernels for 0%

commit v1 on v0

--- a/solution.py
+++ b/solution.py
@@ -290,8 +290,9 @@
                 jnp.concatenate([shift_one, scale_one, gate_one, shift_two, scale_two, gate_two])
             )
         mod_grads[layer_index] = layer_mods
+        track_sides_up = lambda shard_in, a_name: jnp.sum(lax.all_gather(shard_in, a_name), axis=0)
         weight_grads[layer_index] = (
-            lax.psum(terms[0].astype(jnp.bfloat16), "seq").astype(jnp.float32),
+            track_sides_up(terms[0].astype(jnp.bfloat16), "seq").astype(jnp.float32),
             lax.psum(terms[1].astype(jnp.bfloat16), "seq").astype(jnp.float32),
             lax.psum(terms[2].astype(jnp.bfloat16), "seq").astype(jnp.float32),
             lax.psum(terms[3].astype(jnp.bfloat16), "seq").astype(jnp.float32),

time: 4360 us -> 4590 us (1.053)
  waiting for transfers between devices: 3640 us -> 3860 us
    reduce_scatter x8, waiting for transfers between devices: 1640 us -> 1810 us  [reduce_rows(): lax.psum_scatter(product_tn(former, latter).astype(jnp.bfloat16), 'fsdp',...]
    all_gather x1, waiting for transfers between devices: 278 us -> 349 us  [collect(): lax.all_gather(weights[2][layer_index], 'fsdp', axis=0, tiled=True)]
  transfers between devices with their start and end apart: 22 -> 23, of which waited for: 18 -> 19; matrix products, arithmetic and copies ran while one was open for 11% -> 7% of each run, Pallas kernels for 0% -> 0%
where the time goes in v1:
time: 4590 us; the launch traced here: 4580 us
  waiting for transfers between devices  3860 us (84%)
  matrix products  349 us (8%)
  blocking collectives  158 us (3%)
  local copies, waits for them, and re-layouts  106 us (2%)
  other arithmetic  68.2 us (1%)
    reduce_scatter x8, waiting for transfers between devices, reduce_rows(): lax.psum_scatter(product_tn(former, latter).astype(jnp.bfloat16), 'fsdp',...  1810 us
    all_gather x1, waiting for transfers between devices, collect(): lax.all_gather(weights[7][layer_index], 'fsdp', axis=0, tiled=True)  353 us
    all_gather x1, waiting for transfers between devices, collect(): lax.all_gather(weights[3][layer_index], 'fsdp', axis=0, tiled=True)  353 us
    all_gather x1, waiting for transfers between devices, collect(): lax.all_gather(weights[2][layer_index], 'fsdp', axis=0, tiled=True)  349 us
    all_gather x1, waiting for transfers between devices, collect(): lax.all_gather(weights[6][layer_index], 'fsdp', axis=0, tiled=True)  338 us
    all_gather x1, waiting for transfers between devices, collect(): lax.all_gather(weights[4][layer_index], 'fsdp', axis=0, tiled=True)  192 us
    all_gather x1, waiting for transfers between devices, collect(): lax.all_gather(weights[0][layer_index], 'fsdp', axis=0, tiled=True)  187 us
    psum x1, waiting for transfers between devices, per_device(): lax.psum(terms[1].astype(jnp.bfloat16), 'seq').astype(jnp.float32)  156 us
  transfers between devices with their start and end apart: 23, of which 19 were waited for; matrix products, arithmetic and copies ran while one was open for 7% of the time, Pallas kernels for 0%

profile of v1, /device:TPU:0, one launch (start us, length us, event | category | flops | bytes accessed | tf_op | source)
XLA Modules:
  0.0 4579.8 jit_solution(7084917821871566904)
XLA Ops:
  8.7 34.1 all-gather.9
  59.7 61.1 %all-reduce.8.cloned.1.call-done = (f32[8,1,9216]{2,0,1:T(8,128)}, f32[8,1,9216]{2,0,1:T(8,128)}) async-done(((f32[8,1,9216]{2,0,1:T(8,128)}, f32[8,1,9216]{2,0,1:T(8,128)}), (f32[8,1,9216]{2,0,1:T(8,128)}, f32[8,1,9216]{2,0,1:T(8,128)})) %all-reduce.8.cloned.1.call-update) | async-done | bytes 589840
  125.6 191.9 %all-gather.22.cloned.1.call-done = bf16[1,1536,4608]{2,1,0:T(8,128)(2,1)} async-done(((bf16[1,192,4608]{2,1,0:T(8,128)(2,1)}), bf16[1,1536,4608]{2,1,0:T(8,128)(2,1)}) %all-gather.22.cloned.1.call-update) | async-done | bytes 14155792 | tf_op jit(solution)/shard_map/all_gather | solution.py:54
  317.5 8.5 fusion.81
  326.0 187.2 %all-gather.20.cloned.1.call-done = bf16[1,1536,4608]{2,1,0:T(8,128)(2,1)} async-done(((bf16[1,192,4608]{2,1,0:T(8,128)(2,1)}), bf16[1,1536,4608]{2,1,0:T(8,128)(2,1)}) %all-gather.20.cloned.1.call-update) | async-done | bytes 14155792 | tf_op jit(solution)/shard_map/all_gather | solution.py:50
  513.2 9.3 fusion.71
  538.4 32.5 all-to-all-done
  570.8 7.3 copy.63
  578.1 6.4 reshape.498
  595.8 37.9 while.26
  648.4 12.3 all-to-all-done.1
  685.8 348.9 %all-gather.26.cloned.1.call-done = bf16[1,1536,6144]{2,1,0:T(8,128)(2,1)} async-done(((bf16[1,192,6144]{2,1,0:T(8,128)(2,1)}), bf16[1,1536,6144]{2,1,0:T(8,128)(2,1)}) %all-gather.26.cloned.1.call-update) | async-done | bytes 18874384 | tf_op jit(solution)/shard_map/all_gather | solution.py:52
  1034.7 11.2 fusion.61
  1045.9 352.7 %all-gather.28.cloned.1.call-done = bf16[1,6144,1536]{2,1,0:T(8,128)(2,1)} async-done(((bf16[1,768,1536]{2,1,0:T(8,128)(2,1)}), bf16[1,6144,1536]{2,1,0:T(8,128)(2,1)}) %all-gather.28.cloned.1.call-update) | async-done | bytes 18874384 | tf_op jit(solution)/shard_map/all_gather | solution.py:53
  1398.6 13.8 fusion.80
  1412.5 11.9 multiply_reduce_fusion.1
  1425.0 337.6 %all-gather.32.cloned.1.call-done = bf16[1,1536,6144]{2,1,0:T(8,128)(2,1)} async-done(((bf16[1,192,6144]{2,1,0:T(8,128)(2,1)}), bf16[1,1536,6144]{2,1,0:T(8,128)(2,1)}) %all-gather.32.cloned.1.call-update) | async-done | bytes 18874384 | tf_op jit(solution)/shard_map/all_gather | solution.py:56
  1762.6 10.9 fusion.53
  1773.5 353.0 %all-gather.34.cloned.1.call-done = bf16[1,6144,1536]{2,1,0:T(8,128)(2,1)} async-done(((bf16[1,768,1536]{2,1,0:T(8,128)(2,1)}), bf16[1,6144,1536]{2,1,0:T(8,128)(2,1)}) %all-gather.34.cloned.1.call-update) | async-done | bytes 18874384 | tf_op jit(solution)/shard_map/all_gather | solution.py:57
  2126.5 13.1 fusion.141
  2139.6 13.6 multiply_reduce_fusion.7
  2153.9 11.7 fusion.181
  2169.7 15.6 fusion.128
  2192.2 12.9 all-to-all-done.2
  2211.6 82.6 %while.27 = (s32[]{:T(128)}, bf16[6,1184,64]{1,2,0:T(8,128)(2,1)}, bf16[6,1184,64]{1,2,0:T(8,128)(2,1)}, bf16[6,1184,64]{1,2,0:T(8,128)(2,1)}, bf16[6,1184,64]{2...) while((s32[]{:T(128)}, bf16[6,1184,64]{1,2,0:T(8,128)(2,1)}, ...), condition=%wide.region_20.21_spmd, body=%wide.region_18.20_spmd.sunk | while | flops 908553088 | bytes 44910832 | solution.py:262
  2297.9 7.7 copy.76
  2305.7 45.9 %all_to_all.76 = bf16[1184,3,1,384]{3,1,2,0:T(4,128)(2,1)S(1)} all-to-all(bf16[1184,3,1,384]{3,1,2,0:T(4,128)(2,1)} %copy.76), channel_id=1, replica_groups=mesh['seq'=4,'fsdp'=8] {'seq'}, dimensions={0} | all-to-all | bytes 5455872 | tf_op jit(solution)/shard_map/all_to_all | solution.py:269
  2359.4 11.1 convolution_convert_fusion.5
  2385.8 10.1 convolution_convert_fusion.4
  2395.9 11.7 convolution_convert_fusion.3
  2408.3 12.6 convolution_convert_fusion.2
  2421.6 10.5 convolution_convert_fusion.1
  2432.8 10.6 convolution_convert_fusion
  2443.5 155.7 %reduce-scatter.11.cloned.1.call-done = bf16[192,4608]{1,0:T(8,128)(2,1)} async-done(((bf16[1536,4608]{1,0:T(8,128)(2,1)}), bf16[192,4608]{1,0:T(8,128)(2,1)}) %reduce-scatter.11.cloned.1.call-update) | async-done | bytes 1769488 | tf_op jit(solution)/shard_map/reduce_scatter | solution.py:43
  2599.5 10.8 fusion.174
  2610.9 10.9 fusion.121
  2624.3 74.0 %reduce-scatter.13.cloned.1.call-done = bf16[192,1536]{1,0:T(8,128)(2,1)} async-done(((bf16[1536,1536]{1,0:T(8,128)(2,1)}), bf16[192,1536]{1,0:T(8,128)(2,1)}) %reduce-scatter.13.cloned.1.call-update) | async-done | bytes 589840 | tf_op jit(solution)/shard_map/reduce_scatter | solution.py:43
  2698.2 99.4 %reduce-scatter.21.cloned.1.call-done = bf16[192,1536]{1,0:T(8,128)(2,1)} async-done(((bf16[1536,1536]{1,0:T(8,128)(2,1)}), bf16[192,1536]{1,0:T(8,128)(2,1)}) %reduce-scatter.21.cloned.1.call-update) | async-done | bytes 589840 | tf_op jit(solution)/shard_map/reduce_scatter | solution.py:43
  2797.6 232.7 %reduce-scatter.19.cloned.1.call-done = bf16[192,4608]{1,0:T(8,128)(2,1)} async-done(((bf16[1536,4608]{1,0:T(8,128)(2,1)}), bf16[192,4608]{1,0:T(8,128)(2,1)}) %reduce-scatter.19.cloned.1.call-update) | async-done | bytes 1769488 | tf_op jit(solution)/shard_map/reduce_scatter | solution.py:43
  3030.3 312.7 %reduce-scatter.15.cloned.1.call-done = bf16[192,6144]{1,0:T(8,128)(2,1)} async-done(((bf16[1536,6144]{1,0:T(8,128)(2,1)}), bf16[192,6144]{1,0:T(8,128)(2,1)}) %reduce-scatter.15.cloned.1.call-update) | async-done | bytes 2359312 | tf_op jit(solution)/shard_map/reduce_scatter | solution.py:43
  3343.0 312.6 %reduce-scatter.17.cloned.1.call-done = bf16[768,1536]{1,0:T(8,128)(2,1)} async-done(((bf16[6144,1536]{1,0:T(8,128)(2,1)}), bf16[768,1536]{1,0:T(8,128)(2,1)}) %reduce-scatter.17.cloned.1.call-update) | async-done | bytes 2359312 | tf_op jit(solution)/shard_map/reduce_scatter | solution.py:43
  3655.6 312.5 %reduce-scatter.23.cloned.1.call-done = bf16[192,6144]{1,0:T(8,128)(2,1)} async-done(((bf16[1536,6144]{1,0:T(8,128)(2,1)}), bf16[192,6144]{1,0:T(8,128)(2,1)}) %reduce-scatter.23.cloned.1.call-update) | async-done | bytes 2359312 | tf_op jit(solution)/shard_map/reduce_scatter | solution.py:43
  3968.2 312.6 %reduce-scatter.25.cloned.1.call-done = bf16[768,1536]{1,0:T(8,128)(2,1)} async-done(((bf16[6144,1536]{1,0:T(8,128)(2,1)}), bf16[768,1536]{1,0:T(8,128)(2,1)}) %reduce-scatter.25.cloned.1.call-update) | async-done | bytes 2359312 | tf_op jit(solution)/shard_map/reduce_scatter | solution.py:43
  4289.7 15.8 all-reduce.3
  4305.5 31.2 all_gather.57
  4336.7 31.2 all_gather.56
  4388.8 6.0 reduce_sum.310
  4398.8 155.5 %all-reduce.10.cloned.1.call-done = (bf16[1,192,1536]{2,1,0:T(8,128)(2,1)}, bf16[1,192,6144]{2,1,0:T(8,128)(2,1)}, bf16[1,768,1536]{2,1,0:T(8,128)(2,1)}, bf16[1...) async-done(((bf16[1,192,1536]{2,1,0:T(8,128)(2,1)}, bf16[1,192,6144]{2,1,0:T(8,128)(2,1)}, ...) | async-done | bytes 12386320 | tf_op jit(solution)/shard_map/psum | solution.py:296
  (368 shorter events, 312.5 us)
Async XLA Ops:
  7.2 36.6 copy-start
  7.2 113.7 %all-reduce.8.cloned.1.call-start = ((), (), s32[]{:S(2)}) async-start(), calls=%async_computation.30 | async-start | bytes 1179648
  46.4 271.1 %all-gather.22.cloned.1.call-start = ((), (), s32[]{:S(2)}) async-start(), calls=%async_computation.22 | async-start | bytes 15925248 | tf_op jit(solution)/shard_map/all_gather | solution.py:54
  47.2 466.0 %all-gather.20.cloned.1.call-start = ((), (), s32[]{:S(2)}) async-start(), calls=%async_computation.21 | async-start | bytes 15925248 | tf_op jit(solution)/shard_map/all_gather | solution.py:50
  47.9 623.8 %all-gather.30.cloned.1.call-start = ((), (), s32[]{:S(2)}) async-start(), calls=%async_computation.26 | async-start | bytes 5308416 | tf_op jit(solution)/shard_map/all_gather | solution.py:55
  48.5 628.7 %all-gather.24.cloned.1.call-start = ((), (), s32[]{:S(2)}) async-start(), calls=%async_computation.23 | async-start | bytes 5308416 | tf_op jit(solution)/shard_map/all_gather | solution.py:51
  49.1 985.6 %all-gather.26.cloned.1.call-start = ((), (), s32[]{:S(2)}) async-start(), calls=%async_computation.24 | async-start | bytes 21233664 | tf_op jit(solution)/shard_map/all_gather | solution.py:52
  49.7 1349.0 %all-gather.28.cloned.1.call-start = ((), (), s32[]{:S(2)}) async-start(), calls=%async_computation.25 | async-start | bytes 21233664 | tf_op jit(solution)/shard_map/all_gather | solution.py:53
  50.4 1712.2 %all-gather.32.cloned.1.call-start = ((), (), s32[]{:S(2)}) async-start(), calls=%async_computation.27 | async-start | bytes 21233664 | tf_op jit(solution)/shard_map/all_gather | solution.py:56
  51.2 2075.4 %all-gather.34.cloned.1.call-start = ((), (), s32[]{:S(2)}) async-start(), calls=%async_computation.28 | async-start | bytes 21233664 | tf_op jit(solution)/shard_map/all_gather | solution.py:57
  123.3 1289.2 %copy-start.34 = (f32[1536]{0:T(1024)}, f32[1536]{0:T(1024)S(1)}, u32[]{:S(2)}) copy-start(f32[1536]{0:T(1024)S(1)} %get-tuple-element.166) | copy-start | bytes 18436
  125.6 200.3 %copy-start.30 = (f32[1536]{0:T(1024)}, f32[1536]{0:T(1024)S(1)}, u32[]{:S(2)}) copy-start(f32[1536]{0:T(1024)S(1)} %get-tuple-element.163) | copy-start | bytes 18436
  513.2 9.3 copy-start.25
  533.5 37.3 all-to-all-start
  643.1 17.6 all-to-all-start.1
  677.2 7.4 copy-start.70
  677.2 357.5 %copy-start.36 = (f32[1536]{0:T(1024)S(1)}, f32[1536]{0:T(1024)}, u32[]{:S(2)}) copy-start(f32[1536]{0:T(1024)} %get-tuple-element.170) | copy-start | bytes 18436
  1398.6 13.8 copy-start.6
  1398.6 13.8 copy-start.48
  1398.6 13.8 copy-start.56
  1412.5 350.1 %copy-start.28 = (f32[1536]{0:T(1024)S(1)}, f32[1536]{0:T(1024)}, u32[]{:S(2)}) copy-start(f32[1536]{0:T(1024)} %get-tuple-element.160) | copy-start | bytes 18436
  1762.6 363.9 %copy-start.32 = (f32[1536]{0:T(1024)S(1)}, f32[1536]{0:T(1024)}, u32[]{:S(2)}) copy-start(f32[1536]{0:T(1024)} %get-tuple-element.159) | copy-start | bytes 18436
  2153.9 11.7 copy-start.38
  2153.9 15.7 copy-start.73
  2165.6 19.8 slice-start
  2169.7 15.7 slice-start.1
  2169.7 15.7 copy-start.44
  2187.9 17.2 all-to-all-start.2
  2192.2 407.0 %reduce-scatter.11.cloned.1.call-start = ((), (), s32[]{:S(2)}) async-start(), calls=%async_computation.13 | async-start | bytes 15925248 | tf_op jit(solution)/shard_map/reduce_scatter | solution.py:43
  2370.5 327.7 %reduce-scatter.13.cloned.1.call-start = ((), (), s32[]{:S(2)}) async-start(), calls=%async_computation.14 | async-start | bytes 5308416 | tf_op jit(solution)/shard_map/reduce_scatter | solution.py:43
  2376.5 421.2 %reduce-scatter.21.cloned.1.call-start = ((), (), s32[]{:S(2)}) async-start(), calls=%async_computation.18 | async-start | bytes 5308416 | tf_op jit(solution)/shard_map/reduce_scatter | solution.py:43
  2381.9 648.4 %reduce-scatter.19.cloned.1.call-start = ((), (), s32[]{:S(2)}) async-start(), calls=%async_computation.17 | async-start | bytes 15925248 | tf_op jit(solution)/shard_map/reduce_scatter | solution.py:43
  2395.9 947.1 %reduce-scatter.15.cloned.1.call-start = ((), (), s32[]{:S(2)}) async-start(), calls=%async_computation.15 | async-start | bytes 21233664 | tf_op jit(solution)/shard_map/reduce_scatter | solution.py:43
  2407.7 1247.9 %reduce-scatter.17.cloned.1.call-start = ((), (), s32[]{:S(2)}) async-start(), calls=%async_computation.16 | async-start | bytes 21233664 | tf_op jit(solution)/shard_map/reduce_scatter | solution.py:43
  2421.0 1547.2 %reduce-scatter.23.cloned.1.call-start = ((), (), s32[]{:S(2)}) async-start(), calls=%async_computation.19 | async-start | bytes 21233664 | tf_op jit(solution)/shard_map/reduce_scatter | solution.py:43
  2432.1 1848.6 %reduce-scatter.25.cloned.1.call-start = ((), (), s32[]{:S(2)}) async-start(), calls=%async_computation.20 | async-start | bytes 21233664 | tf_op jit(solution)/shard_map/reduce_scatter | solution.py:43
  2443.4 1945.4 %all-gather.36.cloned.1.call-start = ((), (), s32[]{:S(2)}) async-start(), calls=%async_computation.29 | async-start | bytes 8847360 | tf_op jit(solution)/shard_map/all_gather | solution.py:293
  2599.2 11.7 copy-start.41
  2599.2 1955.2 %all-reduce.10.cloned.1.call-start = ((), (), s32[]{:S(2)}) async-start(), calls=%async_computation.31 | async-start | bytes 24772608 | tf_op jit(solution)/shard_map/psum | solution.py:296
  2599.5 11.4 copy-start.1
  2599.5 11.4 copy-start.10
  2599.5 11.4 copy-start.51
  2599.5 11.4 copy-start.60
  2610.9 12.1 copy-start.59
  2610.9 12.7 copy-start.58
  4305.5 63.3 %copy-start.4 = (bf16[1,192,9216]{2,1,0:T(8,128)(2,1)S(1)}, bf16[1,192,9216]{2,1,0:T(8,128)(2,1)}, u32[]{:S(2)}) copy-start(bf16[1,192,9216]{2,1,0:T(8,128)(2,1)} %param.26) | copy-start | bytes 10616836
  4336.7 33.2 copy-start.20
  4370.5 16.1 all-to-all-start.4
  (51 other events, 175.7 us)
Sparse Core Ops, SparseCore 0:
  46.5 74.3 all-reduce.7
  123.1 194.3 all-gather.21
  319.7 193.4 all-gather.19
  515.2 77.4 all-gather.29
  594.8 77.6 all-gather.23
  673.9 360.7 all-gather.25
  1036.2 362.3 all-gather.27
  1400.2 362.3 all-gather.31
  1764.1 362.3 all-gather.33
  2370.6 228.4 reduce-scatter.10
  2603.4 94.8 reduce-scatter.12
  2702.3 95.2 reduce-scatter.20
  2801.3 229.0 reduce-scatter.18
  3034.1 308.8 reduce-scatter.14
  3346.7 308.8 reduce-scatter.16
  3659.3 308.7 reduce-scatter.22
  3971.9 308.8 reduce-scatter.24
  4282.2 51.2 all-gather.35
  4336.7 217.5 all-reduce.9
